TPU v7x, 512 devices: a whole 4x4x16 slice. The times are simulated.
512 devices in a mesh: sec: 2 (over z_hi), gx: 16 (over z_lo, core), gy: 16 (over x, y).
Axes of the slice: x: 4, y: 4, z: 16 (z_hi: 2, z_lo: 8; z = z_hi * 8 + z_lo), core: 2. Of those that a mesh axis runs over, the one named last changes fastest.
Arguments:
- terminal: float32 [4, 16, 256, 4096], P('sec', None, 'gx', 'gy'), may hold values from -6 to 6
- forward_temp: bfloat16 [2, 4, 16, 256, 4096], P(None, 'sec', None, 'gx', 'gy'), may hold values from -6 to 6
- conductivity: float32 [16, 256, 4096], P(None, 'gx', 'gy'), may hold values from 0.02 to 0.15
- velocity: float32 [2, 16, 256, 4096], P(None, None, 'gx', 'gy'), may hold values from -0.3 to 0.3
- fixed_mask: int32 [16, 256, 4096], P(None, 'gx', 'gy'), may hold values 0 or 1
- wells: int32 [4, 8, 3], P('sec'), may hold values from 0 to 4095, as said below
- misfit: float32 [2, 4, 8], P(None, 'sec'), may hold values from -12 to 12
- head_gradient: bfloat16 [2, 16, 256, 4096], P('sec', None, 'gx', 'gy'), may hold values from -6 to 6
- blocks: bfloat16 [32, 7, 128, 128], P('gy'), may hold values from -0.1875 to 0.1875
- block_cols: int32 [32, 7], P('gy'), may hold values from 0 to 31, as said below
Outputs:
- head_adjoint: float32 [2, 16, 256, 4096], P('sec', None, 'gx', 'gy')
- sensitivity: float32 [16, 256, 4096], P(None, 'gx', 'gy')
Inputs may be any that keep to these rules, and one draw needn't show every extreme that they name: `wells`: each row is one cell (z, x, y) with z < 16, x < 256, y < 4096; the first test observes the cells (0, 0, 0) and (15, 255, 4095). `block_cols`: row r lists 7 different block columns, the first of which is r.
All inputs are finite; a program needn't handle non-finite values. No bound on the sum of `fixed_mask` on one device may be relied on, other than what follows from the above.
Results may differ from a plain program's by a relative error of at most 0.0029.
Values may be sent and summed in bfloat16 or wider, within the bound.
No kernel may reach another device: no remote copies, remote signals or barrier semaphores. Data moves between devices by JAX's collectives and lax.ppermute only.
A program may use at most 64 MiB of HBM per device.

v0:
```python
import jax
import jax.numpy as jnp
from jax import lax
from jax.sharding import PartitionSpec as P


def extended(cells, sides, width):
    for axis, dim in sides:
        count = lax.axis_size(axis)
        ends = count - 1
        head = lax.slice_in_dim(cells, 0, width, axis=dim)
        tail = lax.slice_in_dim(cells, cells.shape[dim] - width, cells.shape[dim], axis=dim)
        cells = jnp.concatenate(
            [
                lax.ppermute(tail, axis, [(i, (i + 1) % count) for i in range(ends)]),
                cells,
                lax.ppermute(head, axis, [((i + 1) % count, i) for i in range(ends)]),
            ],
            axis=dim,
        )
    return cells


def shifted(padded):
    lead = [(0, 0)] * (padded.ndim - 3)
    deeper = jnp.pad(padded, lead + [(1, 1), (0, 0), (0, 0)])
    centre = deeper[..., 1:-1, 1:-1, 1:-1]
    beside_all = [
        deeper[..., 2:, 1:-1, 1:-1],
        deeper[..., :-2, 1:-1, 1:-1],
        deeper[..., 1:-1, 2:, 1:-1],
        deeper[..., 1:-1, :-2, 1:-1],
        deeper[..., 1:-1, 1:-1, 2:],
        deeper[..., 1:-1, 1:-1, :-2],
    ]
    return (centre, beside_all)


def face_weights(kappa_pad):
    centre, beside_all = shifted(kappa_pad)
    return [
        2.0 * centre * other / jnp.where(centre + other > 0.0, centre + other, 1.0)
        for other in beside_all
    ]


def advance(adjoint_pad, weights, keep, speed_x, speed_y, source):
    centre, beside_all = shifted(adjoint_pad)
    diffusion = weights[0] * (beside_all[0] - centre)
    for face in range(1, 6):
        diffusion = diffusion + weights[face] * (beside_all[face] - centre)
    slope_x = 0.5 * (beside_all[2] - beside_all[3])
    slope_y = 0.5 * (beside_all[4] - beside_all[5])
    updated = keep * (centre + diffusion + speed_x * slope_x + speed_y * slope_y + source)
    return (updated, diffusion, slope_x, slope_y)


def well_sources(wells, misfit_level, layers, rows_x, cols_y, margin):
    start_x = lax.axis_index("gx") * rows_x - margin
    start_y = lax.axis_index("gy") * cols_y - margin
    coord_z = jnp.arange(layers, dtype=jnp.int32)[:, None, None]
    coord_x = (start_x + jnp.arange(rows_x + 2 * margin, dtype=jnp.int32))[None, :, None]
    coord_y = (start_y + jnp.arange(cols_y + 2 * margin, dtype=jnp.int32))[None, None, :]
    well_z = wells[:, :, 0][:, :, None, None, None]
    well_x = wells[:, :, 1][:, :, None, None, None]
    well_y = wells[:, :, 2][:, :, None, None, None]
    matches = (coord_z == well_z) & (coord_x == well_x) & (coord_y == well_y)
    return jnp.sum(jnp.where(matches, misfit_level[:, :, None, None, None], 0.0), axis=1)


def shards(
    terminal,
    forward_temp,
    conductivity,
    velocity,
    fixed_mask,
    wells,
    misfit,
    head_gradient,
    blocks,
    block_cols,
):
    layers, rows_x, cols_y = conductivity.shape
    steps = forward_temp.shape[0]
    keep = 1.0 - fixed_mask.astype(jnp.float32)
    heat_sens = jnp.zeros((layers, rows_x, cols_y), jnp.float32)
    flow_x = jnp.zeros((layers, rows_x, cols_y), jnp.float32)
    flow_y = jnp.zeros((layers, rows_x, cols_y), jnp.float32)
    kappa_pad = extended(conductivity, (("gx", 1), ("gy", 2)), 1)
    weights = face_weights(kappa_pad)
    adjoint = terminal
    for level in reversed(range(steps)):
        padded = extended(adjoint, (("gx", 2), ("gy", 3)), 1)
        source = well_sources(wells, misfit[level], layers, rows_x, cols_y, 0)
        adjoint, diffusion, slope_x, slope_y = advance(
            padded, weights, keep, velocity[0], velocity[1], source
        )
        temper = forward_temp[level].astype(jnp.float32)
        heat_sens = heat_sens + jnp.sum(temper * diffusion, axis=0)
        flow_x = flow_x + jnp.sum(temper * slope_x, axis=0)
        flow_y = flow_y + jnp.sum(temper * slope_y, axis=0)
    summed = lax.psum_scatter(jnp.stack([flow_x, flow_y]), "sec", scatter_dimension=0, tiled=True)
    rounded = summed[0].astype(jnp.bfloat16)
    row_blocks, per_row, block_size, _ = blocks.shape
    piece = lax.all_gather(rounded, "gy", axis=2, tiled=True)
    count = piece.shape[2] // block_size
    split_rows = piece.reshape(layers, rows_x, count, block_size)
    block_ids = jnp.arange(count, dtype=jnp.int32)
    chosen = (block_cols[:, :, None] == block_ids[None, None, :]).astype(jnp.bfloat16)
    portion = jnp.einsum("bkq,zxqj->bkzxj", chosen, split_rows, preferred_element_type=jnp.float32)
    picked = portion.astype(jnp.bfloat16)
    head = jnp.einsum(
        "bkzxj,bkij->zxbi", picked, blocks, preferred_element_type=jnp.float32
    ).reshape(layers, rows_x, cols_y)
    partial_sens = heat_sens + head * head_gradient[0].astype(jnp.float32)
    sensitivity = lax.psum(partial_sens, "sec")
    return (head[None], sensitivity)


def solution(mesh):
    placed = (
        P("sec", None, "gx", "gy"),
        P(None, "sec", None, "gx", "gy"),
        P(None, "gx", "gy"),
        P(None, None, "gx", "gy"),
        P(None, "gx", "gy"),
        P("sec", None, None),
        P(None, "sec", None),
        P("sec", None, "gx", "gy"),
        P("gy", None, None, None),
        P("gy", None),
    )
    return jax.shard_map(
        shards,
        mesh=mesh,
        in_specs=placed,
        out_specs=(P("sec", None, "gx", "gy"), P(None, "gx", "gy")),
        check_vma=False,
    )
```

profile of v0, /device:TPU:1, one launch (start us, length us, event | category | flops | bytes accessed | tf_op | source)
XLA Modules:
  0.0 278.9 jit_solution(739867863807899032)
XLA Ops:
  8.3 4.9 %collective-permute-start.2 = (f32[16,1,256]{2,1,0:T(1,128)S(1)}, f32[16,1,256]{2,1,0:T(1,128)S(1)}, u32[]{:S(2)}, u32[]{:S(2)}) collective-permute-start(f32[16,1,256]{2,1,0:T(1,128)S(1)} %get-tuple-element.29), channel_id=1, source_target_pairs={{0,16},{16,32},{32,48},{48,64},{64,80},{80,96},{96,112},{112,128},... | collective-permute-start | bytes 49160 | tf_op jit(solution)/shard_map/ppermute | solution.py:15
  13.3 5.1 %collective-permute-start.3 = (f32[16,1,256]{2,1,0:T(1,128)S(1)}, f32[16,1,256]{2,1,0:T(1,128)S(1)}, u32[]{:S(2)}, u32[]{:S(2)}) collective-permute-start(f32[16,1,256]{2,1,0:T(1,128)S(1)} %get-tuple-element.30), channel_id=1, source_target_pairs={{16,0},{32,16},{48,32},{64,48},{80,64},{96,80},{112,96},{128,112},... | collective-permute-start | bytes 49160 | tf_op jit(solution)/shard_map/ppermute | solution.py:17
  19.5 1.9 collective-permute-start
  21.4 3.6 %collective-permute-start.1 = (f32[2,16,1,256]{3,2,1,0:T(1,128)S(1)}, f32[2,16,1,256]{3,2,1,0:T(1,128)S(1)}, u32[]{:S(2)}, u32[]{:S(2)}) collective-permute-start(f32[2,16,1,256]{3,2,1,0:T(1,128)S(1)} %get-tuple-element.20), channel_id=1, source_target_pairs={{0,16},{16,32},{32,48},{48,64},{64,80},{80,96},{96,112},{112,128},... | collective-permute-start | bytes 98312 | tf_op jit(solution)/shard_map/ppermute | solution.py:15
  27.5 1.4 collective-permute-start.4
  28.9 1.3 collective-permute-start.5
  31.1 1.5 collective-permute-done.4
  32.6 4.1 %collective-permute-done.5 = f32[16,18,1]{2,1,0:T(8,128)S(1)} collective-permute-done((f32[16,18,1]{2,1,0:T(8,128)S(1)}, f32[16,18,1]{2,1,0:T(8,128)S(1)}, u32[]{:S(2)}, u32[]{:S(2)}) %collective-permute-start.5) | collective-permute-done | bytes 1184 | tf_op jit(solution)/shard_map/ppermute | solution.py:17
  37.4 2.2 collective-permute-start.6
  41.5 6.3 %collective-permute-done.6 = f32[2,16,18,1]{3,2,1,0:T(8,128)S(1)} collective-permute-done((f32[2,16,18,1]{3,2,1,0:T(8,128)S(1)}, f32[2,16,18,1]{3,2,1,0:T(8,128)S(1)}, u32[]{:S(2)}, u32[]{:S(2)}) %collective-permute-start.6) | collective-permute-done | bytes 2336 | tf_op jit(solution)/shard_map/ppermute | solution.py:15
  47.8 3.8 %collective-permute-done.7 = f32[2,16,18,1]{3,2,1,0:T(8,128)S(1)} collective-permute-done((f32[2,16,18,1]{3,2,1,0:T(8,128)S(1)}, f32[2,16,18,1]{3,2,1,0:T(8,128)S(1)}, u32[]{:S(2)}, u32[]{:S(2)}) %collective-permute-start.7) | collective-permute-done | bytes 2336 | tf_op jit(solution)/shard_map/ppermute | solution.py:17
  53.5 3.3 %collective-permute-start.8 = (f32[2,16,1,256]{3,2,1,0:T(1,128)S(1)}, f32[2,16,1,256]{3,2,1,0:T(1,128)S(1)}, u32[]{:S(2)}, u32[]{:S(2)}) collective-permute-start(f32[2,16,1,256]{3,2,1,0:T(1,128)S(1)} %get-tuple-element.15), channel_id=1, source_target_pairs={{16,0},{32,16},{48,32},{64,48},{80,64},{96,80},{112,96},{128,112},... | collective-permute-start | bytes 98312 | tf_op jit(solution)/shard_map/ppermute | solution.py:17
  56.8 3.8 %collective-permute-start.9 = (f32[2,16,1,256]{3,2,1,0:T(1,128)S(1)}, f32[2,16,1,256]{3,2,1,0:T(1,128)S(1)}, u32[]{:S(2)}, u32[]{:S(2)}) collective-permute-start(f32[2,16,1,256]{3,2,1,0:T(1,128)S(1)} %get-tuple-element.16), channel_id=1, source_target_pairs={{0,16},{16,32},{32,48},{48,64},{64,80},{80,96},{96,112},{112,128},... | collective-permute-start | bytes 98312 | tf_op jit(solution)/shard_map/ppermute | solution.py:15
  63.2 5.1 %collective-permute-start.11 = (f32[2,16,18,1]{3,2,1,0:T(8,128)S(1)}, f32[2,16,18,1]{3,2,1,0:T(8,128)S(1)}, u32[]{:S(2)}, u32[]{:S(2)}) collective-permute-start(f32[2,16,18,1]{3,2,1,0:T(8,128)S(1)} %get-tuple-element.12), channel_id=1, source_target_pairs={{0,1},{1,2},{2,3},{3,4},{4,5},{5,6},{6,7},{7,8},{8,9},{9,10},{10,1... | collective-permute-start | bytes 6920 | tf_op jit(solution)/shard_map/ppermute | solution.py:15
  68.9 5.6 %collective-permute-done.10 = f32[2,16,18,1]{3,2,1,0:T(8,128)S(1)} collective-permute-done((f32[2,16,18,1]{3,2,1,0:T(8,128)S(1)}, f32[2,16,18,1]{3,2,1,0:T(8,128)S(1)}, u32[]{:S(2)}, u32[]{:S(2)}) %collective-permute-start.10) | collective-permute-done | bytes 2336 | tf_op jit(solution)/shard_map/ppermute | solution.py:17
  74.5 1.8 collective-permute-done.11
  76.2 1.3 fusion.7
  78.5 59.7 %reduce-scatter.2.cloned.1.call-done = f32[1,16,16,256]{3,2,1,0:T(8,128)} async-done(((f32[2,16,16,256]{3,2,1,0:T(8,128)}), f32[1,16,16,256]{3,2,1,0:T(8,128)}) %reduce-scatter.2.cloned.1.call-update) | async-done | bytes 262160 | tf_op jit(solution)/shard_map/reduce_scatter | solution.py:102
  138.3 1.6 convert_element_type.41
  141.0 1.7 fusion.9
  142.7 52.4 %all-gather.3.cloned.1.call-done = bf16[1,16,16,4096]{3,2,1,0:T(8,128)(2,1)} async-done(((bf16[1,16,16,256]{3,2,1,0:T(8,128)(2,1)}), bf16[1,16,16,4096]{3,2,1,0:T(8,128)(2,1)}) %all-gather.3.cloned.1.call-update) | async-done | bytes 2097168 | tf_op jit(solution)/shard_map/all_gather | solution.py:105
  195.1 2.1 copy.21
  200.7 70.0 %all-reduce.5.cloned.1.call-done = f32[16,16,256]{2,1,0:T(8,128)} async-done(((f32[16,16,256]{2,1,0:T(8,128)}), f32[16,16,256]{2,1,0:T(8,128)}) %all-reduce.5.cloned.1.call-update) | async-done | bytes 262160 | tf_op jit(solution)/shard_map/psum | solution.py:116
  270.7 1.7 copy.26
  (69 shorter events, 18.4 us)
Async XLA Ops:
  7.2 190.6 %copy-start = (bf16[2,7,128,128]{3,2,1,0:T(8,128)(2,1)S(1)}, bf16[2,7,128,128]{3,2,1,0:T(8,128)(2,1)}, u32[]{:S(2)}) copy-start(bf16[2,7,128,128]{3,2,1,0:T(8,128)(2,1)} %param.18) | copy-start | bytes 1376260
  7.2 20.1 %copy-start.2 = (f32[16,16,256]{2,1,0:T(8,128)S(1)}, f32[16,16,256]{2,1,0:T(8,128)}, u32[]{:S(2)}) copy-start(f32[16,16,256]{2,1,0:T(8,128)} %param.12) | copy-start | bytes 786436
  7.2 19.8 %copy-start.7 = (s32[16,16,256]{2,1,0:T(8,128)S(1)}, s32[16,16,256]{2,1,0:T(8,128)}, u32[]{:S(2)}) copy-start(s32[16,16,256]{2,1,0:T(8,128)} %param.14) | copy-start | bytes 786436
  7.2 20.1 %copy-start.10 = (f32[2,2,8]{2,1,0:T(2,128)S(1)}, f32[2,2,8]{2,1,0:T(2,128)}, u32[]{:S(2)}) copy-start(f32[2,2,8]{2,1,0:T(2,128)} %param.16) | copy-start | bytes 388
  7.2 131.1 %reduce-scatter.2.cloned.1.call-start = ((), (), s32[]{:S(2)}) async-start(), calls=%async_computation.1 | async-start | bytes 786432 | tf_op jit(solution)/shard_map/reduce_scatter | solution.py:102
  8.3 18.9 %collective-permute-start.2 = (f32[16,1,256]{2,1,0:T(1,128)S(1)}, f32[16,1,256]{2,1,0:T(1,128)S(1)}, u32[]{:S(2)}, u32[]{:S(2)}) collective-permute-start(f32[16,1,256]{2,1,0:T(1,128)S(1)} %get-tuple-element.29), channel_id=1, source_target_pairs={{0,16},{16,32},{32,48},{48,64},{64,80},{80,96},{96,112},{112,128},... | collective-permute-start | bytes 49160 | tf_op jit(solution)/shard_map/ppermute | solution.py:15
  13.3 14.0 %collective-permute-start.3 = (f32[16,1,256]{2,1,0:T(1,128)S(1)}, f32[16,1,256]{2,1,0:T(1,128)S(1)}, u32[]{:S(2)}, u32[]{:S(2)}) collective-permute-start(f32[16,1,256]{2,1,0:T(1,128)S(1)} %get-tuple-element.30), channel_id=1, source_target_pairs={{16,0},{32,16},{48,32},{64,48},{80,64},{96,80},{112,96},{128,112},... | collective-permute-start | bytes 49160 | tf_op jit(solution)/shard_map/ppermute | solution.py:17
  19.5 17.6 %collective-permute-start = (f32[2,16,1,256]{3,2,1,0:T(1,128)S(1)}, f32[2,16,1,256]{3,2,1,0:T(1,128)S(1)}, u32[]{:S(2)}, u32[]{:S(2)}) collective-permute-start(f32[2,16,1,256]{3,2,1,0:T(1,128)S(1)} %get-tuple-element.19), channel_id=1, source_target_pairs={{16,0},{32,16},{48,32},{64,48},{80,64},{96,80},{112,96},{128,112},... | collective-permute-start | bytes 98312 | tf_op jit(solution)/shard_map/ppermute | solution.py:17
  21.4 15.7 %collective-permute-start.1 = (f32[2,16,1,256]{3,2,1,0:T(1,128)S(1)}, f32[2,16,1,256]{3,2,1,0:T(1,128)S(1)}, u32[]{:S(2)}, u32[]{:S(2)}) collective-permute-start(f32[2,16,1,256]{3,2,1,0:T(1,128)S(1)} %get-tuple-element.20), channel_id=1, source_target_pairs={{0,16},{16,32},{32,48},{48,64},{64,80},{80,96},{96,112},{112,128},... | collective-permute-start | bytes 98312 | tf_op jit(solution)/shard_map/ppermute | solution.py:15
  27.4 9.7 %copy-start.1 = (f32[2,16,16,256]{3,2,1,0:T(8,128)S(1)}, f32[2,16,16,256]{3,2,1,0:T(8,128)}, u32[]{:S(2)}) copy-start(f32[2,16,16,256]{3,2,1,0:T(8,128)} %param.10) | copy-start | bytes 1572868
  27.5 5.1 %collective-permute-start.4 = (f32[16,18,1]{2,1,0:T(8,128)S(1)}, f32[16,18,1]{2,1,0:T(8,128)S(1)}, u32[]{:S(2)}, u32[]{:S(2)}) collective-permute-start(f32[16,18,1]{2,1,0:T(8,128)S(1)} %get-tuple-element.22), channel_id=1, source_target_pairs={{0,1},{1,2},{2,3},{3,4},{4,5},{5,6},{6,7},{7,8},{8,9},{9,10},{10,1... | collective-permute-start | bytes 3464 | tf_op jit(solution)/shard_map/ppermute | solution.py:15
  28.9 7.8 %collective-permute-start.5 = (f32[16,18,1]{2,1,0:T(8,128)S(1)}, f32[16,18,1]{2,1,0:T(8,128)S(1)}, u32[]{:S(2)}, u32[]{:S(2)}) collective-permute-start(f32[16,18,1]{2,1,0:T(8,128)S(1)} %get-tuple-element.21), channel_id=1, source_target_pairs={{1,0},{2,1},{3,2},{4,3},{5,4},{6,5},{7,6},{8,7},{9,8},{10,9},{11,1... | collective-permute-start | bytes 3464 | tf_op jit(solution)/shard_map/ppermute | solution.py:17
  37.4 10.4 %collective-permute-start.6 = (f32[2,16,18,1]{3,2,1,0:T(8,128)S(1)}, f32[2,16,18,1]{3,2,1,0:T(8,128)S(1)}, u32[]{:S(2)}, u32[]{:S(2)}) collective-permute-start(f32[2,16,18,1]{3,2,1,0:T(8,128)S(1)} %get-tuple-element.14), channel_id=1, source_target_pairs={{0,1},{1,2},{2,3},{3,4},{4,5},{5,6},{6,7},{7,8},{8,9},{9,10},{10,1... | collective-permute-start | bytes 6920 | tf_op jit(solution)/shard_map/ppermute | solution.py:15
  39.6 12.0 %collective-permute-start.7 = (f32[2,16,18,1]{3,2,1,0:T(8,128)S(1)}, f32[2,16,18,1]{3,2,1,0:T(8,128)S(1)}, u32[]{:S(2)}, u32[]{:S(2)}) collective-permute-start(f32[2,16,18,1]{3,2,1,0:T(8,128)S(1)} %get-tuple-element.13), channel_id=1, source_target_pairs={{1,0},{2,1},{3,2},{4,3},{5,4},{6,5},{7,6},{8,7},{9,8},{10,9},{11,1... | collective-permute-start | bytes 6920 | tf_op jit(solution)/shard_map/ppermute | solution.py:17
  53.5 7.1 %collective-permute-start.8 = (f32[2,16,1,256]{3,2,1,0:T(1,128)S(1)}, f32[2,16,1,256]{3,2,1,0:T(1,128)S(1)}, u32[]{:S(2)}, u32[]{:S(2)}) collective-permute-start(f32[2,16,1,256]{3,2,1,0:T(1,128)S(1)} %get-tuple-element.15), channel_id=1, source_target_pairs={{16,0},{32,16},{48,32},{64,48},{80,64},{96,80},{112,96},{128,112},... | collective-permute-start | bytes 98312 | tf_op jit(solution)/shard_map/ppermute | solution.py:17
  56.8 11.5 %copy-start.3 = (bf16[2,2,16,16,256]{4,3,2,1,0:T(8,128)(2,1)S(1)}, bf16[2,2,16,16,256]{4,3,2,1,0:T(8,128)(2,1)}, u32[]{:S(2)}) copy-start(bf16[2,2,16,16,256]{4,3,2,1,0:T(8,128)(2,1)} %param.11) | copy-start | bytes 1572868
  56.8 4.8 %collective-permute-start.9 = (f32[2,16,1,256]{3,2,1,0:T(1,128)S(1)}, f32[2,16,1,256]{3,2,1,0:T(1,128)S(1)}, u32[]{:S(2)}, u32[]{:S(2)}) collective-permute-start(f32[2,16,1,256]{3,2,1,0:T(1,128)S(1)} %get-tuple-element.16), channel_id=1, source_target_pairs={{0,16},{16,32},{32,48},{48,64},{64,80},{80,96},{96,112},{112,128},... | collective-permute-start | bytes 98312 | tf_op jit(solution)/shard_map/ppermute | solution.py:15
  61.9 12.6 %collective-permute-start.10 = (f32[2,16,18,1]{3,2,1,0:T(8,128)S(1)}, f32[2,16,18,1]{3,2,1,0:T(8,128)S(1)}, u32[]{:S(2)}, u32[]{:S(2)}) collective-permute-start(f32[2,16,18,1]{3,2,1,0:T(8,128)S(1)} %get-tuple-element.11), channel_id=1, source_target_pairs={{1,0},{2,1},{3,2},{4,3},{5,4},{6,5},{7,6},{8,7},{9,8},{10,9},{11,1... | collective-permute-start | bytes 6920 | tf_op jit(solution)/shard_map/ppermute | solution.py:17
  63.2 13.0 %collective-permute-start.11 = (f32[2,16,18,1]{3,2,1,0:T(8,128)S(1)}, f32[2,16,18,1]{3,2,1,0:T(8,128)S(1)}, u32[]{:S(2)}, u32[]{:S(2)}) collective-permute-start(f32[2,16,18,1]{3,2,1,0:T(8,128)S(1)} %get-tuple-element.12), channel_id=1, source_target_pairs={{0,1},{1,2},{2,3},{3,4},{4,5},{5,6},{6,7},{7,8},{8,9},{9,10},{10,1... | collective-permute-start | bytes 6920 | tf_op jit(solution)/shard_map/ppermute | solution.py:15
  78.5 116.6 %all-gather.3.cloned.1.call-start = ((), (), s32[]{:S(2)}) async-start(), calls=%async_computation.3 | async-start | bytes 2228224 | tf_op jit(solution)/shard_map/all_gather | solution.py:105
  139.9 130.8 %all-reduce.5.cloned.1.call-start = ((), (), s32[]{:S(2)}) async-start(), calls=%async_computation.2 | async-start | bytes 524288 | tf_op jit(solution)/shard_map/psum | solution.py:116
  140.0 1.0 copy-start.4
  195.1 2.1 copy-start.9
  197.8 1.0 copy-start.8
  (2 other events, 2.0 us)
Sparse Core Ops, SparseCore 0:
  78.6 59.6 reduce-scatter.1
  141.7 53.3 all-gather.2
  199.7 70.9 all-reduce.4
where the time goes:
time: 280 us; the launch traced here: 279 us
  waiting for transfers between devices  206 us (74%)
  starting transfers between devices  35.4 us (13%)
  between operations  14.1 us (5%)
  other arithmetic  12.9 us (5%)
  local copies, waits for them, and re-layouts  9.19 us (3%)
    psum x1, waiting for transfers between devices, shards(): sensitivity = lax.psum(partial_sens, 'sec')  70 us
    reduce_scatter x1, waiting for transfers between devices, shards(): lax.psum_scatter(jnp.stack([flow_x, flow_y]), 'sec', scatter_dimension=0,...  59.7 us
    all_gather x1, waiting for transfers between devices, shards(): piece = lax.all_gather(rounded, 'gy', axis=2, tiled=True)  52.4 us
    ppermute x6, starting transfers between devices, extended(): lax.ppermute(tail, axis, [(i, (i + 1) % count) for i in range(ends)])  21 us
    ppermute x6, starting transfers between devices, extended(): lax.ppermute(head, axis, [((i + 1) % count, i) for i in range(ends)])  14.3 us
    ppermute x6, waiting for transfers between devices, extended(): lax.ppermute(head, axis, [((i + 1) % count, i) for i in range(ends)])  13.5 us
    ppermute x6, waiting for transfers between devices, extended(): lax.ppermute(tail, axis, [(i, (i + 1) % count) for i in range(ends)])  10.6 us
  transfers between devices with their start and end apart: 15, of which 10 were waited for; matrix products, arithmetic and copies ran while one was open for 3% of the time, Pallas kernels for 0%

commit v1 on v0

--- a/solution.py
+++ b/solution.py
@@ -102,7 +102,9 @@
     summed = lax.psum_scatter(jnp.stack([flow_x, flow_y]), "sec", scatter_dimension=0, tiled=True)
     rounded = summed[0].astype(jnp.bfloat16)
     row_blocks, per_row, block_size, _ = blocks.shape
-    piece = lax.all_gather(rounded, "gy", axis=2, tiled=True)
+    piece = jnp.concatenate(
+        lax.all_to_all(jnp.stack([rounded] * lax.axis_size("gy")), "gy", 0, 0), axis=2
+    )
     count = piece.shape[2] // block_size
     split_rows = piece.reshape(layers, rows_x, count, block_size)
     block_ids = jnp.arange(count, dtype=jnp.int32)

time: 280 us -> 254 us (0.907)
  waiting for transfers between devices: 206 us -> 169 us
  starting transfers between devices: 35.4 us -> 41.9 us
  local copies, waits for them, and re-layouts: 9.19 us -> 13.6 us
    all_gather x1 -> x0, waiting for transfers between devices: 52.4 us -> none  [shards(): piece = lax.all_gather(rounded, 'gy', axis=2, tiled=True)]
    all_to_all x0 -> x1, waiting for transfers between devices: none -> 24.3 us  [shards(): lax.all_to_all(jnp.stack([rounded] * lax.axis_size('gy')), 'gy', 0, 0)]
    psum x1, waiting for transfers between devices: 70 us -> 60.4 us  [shards(): sensitivity = lax.psum(partial_sens, 'sec')]
    all_to_all x0 -> x1, starting transfers between devices: none -> 6.53 us  [shards(): lax.all_to_all(jnp.stack([rounded] * lax.axis_size('gy')), 'gy', 0, 0)]
    another operation x0 -> x2, local copies, waits for them, and re-layouts: none -> 4.24 us  [the longest x1 2.69 us: shards(): split_rows = piece.reshape(layers, rows_x, count, block_size)]
  transfers between devices with their start and end apart: 15 -> 15, of which waited for: 10 -> 10; matrix products, arithmetic and copies ran while one was open for 3% -> 4% of each run, Pallas kernels for 0% -> 0%
where the time goes in v1:
time: 254 us; the launch traced here: 253 us
  waiting for transfers between devices  169 us (67%)
  starting transfers between devices  41.9 us (16%)
  between operations  14.7 us (6%)
  local copies, waits for them, and re-layouts  13.6 us (5%)
  other arithmetic  13.4 us (5%)
    psum x1, waiting for transfers between devices, shards(): sensitivity = lax.psum(partial_sens, 'sec')  60.4 us
    reduce_scatter x1, waiting for transfers between devices, shards(): lax.psum_scatter(jnp.stack([flow_x, flow_y]), 'sec', scatter_dimension=0,...  59.8 us
    all_to_all x1, waiting for transfers between devices, shards(): lax.all_to_all(jnp.stack([rounded] * lax.axis_size('gy')), 'gy', 0, 0)  24.3 us
    ppermute x6, starting transfers between devices, extended(): lax.ppermute(tail, axis, [(i, (i + 1) % count) for i in range(ends)])  21 us
    ppermute x6, starting transfers between devices, extended(): lax.ppermute(head, axis, [((i + 1) % count, i) for i in range(ends)])  14.3 us
    ppermute x6, waiting for transfers between devices, extended(): lax.ppermute(head, axis, [((i + 1) % count, i) for i in range(ends)])  13.5 us
    ppermute x6, waiting for transfers between devices, extended(): lax.ppermute(tail, axis, [(i, (i + 1) % count) for i in range(ends)])  10.5 us
    all_to_all x1, starting transfers between devices, shards(): lax.all_to_all(jnp.stack([rounded] * lax.axis_size('gy')), 'gy', 0, 0)  6.53 us
  transfers between devices with their start and end apart: 15, of which 10 were waited for; matrix products, arithmetic and copies ran while one was open for 4% of the time, Pallas kernels for 0%

profile of v1, /device:TPU:1, one launch (start us, length us, event | category | flops | bytes accessed | tf_op | source)
XLA Modules:
  0.0 253.2 jit_solution(18214689588705697450)
XLA Ops:
  8.3 4.9 %collective-permute-start.2 = (f32[16,1,256]{2,1,0:T(1,128)S(1)}, f32[16,1,256]{2,1,0:T(1,128)S(1)}, u32[]{:S(2)}, u32[]{:S(2)}) collective-permute-start(f32[16,1,256]{2,1,0:T(1,128)S(1)} %get-tuple-element.29), channel_id=1, source_target_pairs={{0,16},{16,32},{32,48},{48,64},{64,80},{80,96},{96,112},{112,128},... | collective-permute-start | bytes 49160 | tf_op jit(solution)/shard_map/ppermute | solution.py:15
  13.3 5.1 %collective-permute-start.3 = (f32[16,1,256]{2,1,0:T(1,128)S(1)}, f32[16,1,256]{2,1,0:T(1,128)S(1)}, u32[]{:S(2)}, u32[]{:S(2)}) collective-permute-start(f32[16,1,256]{2,1,0:T(1,128)S(1)} %get-tuple-element.30), channel_id=1, source_target_pairs={{16,0},{32,16},{48,32},{64,48},{80,64},{96,80},{112,96},{128,112},... | collective-permute-start | bytes 49160 | tf_op jit(solution)/shard_map/ppermute | solution.py:17
  19.5 1.9 collective-permute-start
  21.4 3.6 %collective-permute-start.1 = (f32[2,16,1,256]{3,2,1,0:T(1,128)S(1)}, f32[2,16,1,256]{3,2,1,0:T(1,128)S(1)}, u32[]{:S(2)}, u32[]{:S(2)}) collective-permute-start(f32[2,16,1,256]{3,2,1,0:T(1,128)S(1)} %get-tuple-element.20), channel_id=1, source_target_pairs={{0,16},{16,32},{32,48},{48,64},{64,80},{80,96},{96,112},{112,128},... | collective-permute-start | bytes 98312 | tf_op jit(solution)/shard_map/ppermute | solution.py:15
  31.1 1.5 collective-permute-done.4
  32.6 4.1 %collective-permute-done.5 = f32[16,18,1]{2,1,0:T(8,128)S(1)} collective-permute-done((f32[16,18,1]{2,1,0:T(8,128)S(1)}, f32[16,18,1]{2,1,0:T(8,128)S(1)}, u32[]{:S(2)}, u32[]{:S(2)}) %collective-permute-start.5) | collective-permute-done | bytes 1184 | tf_op jit(solution)/shard_map/ppermute | solution.py:17
  37.4 2.2 collective-permute-start.6
  41.5 6.3 %collective-permute-done.6 = f32[2,16,18,1]{3,2,1,0:T(8,128)S(1)} collective-permute-done((f32[2,16,18,1]{3,2,1,0:T(8,128)S(1)}, f32[2,16,18,1]{3,2,1,0:T(8,128)S(1)}, u32[]{:S(2)}, u32[]{:S(2)}) %collective-permute-start.6) | collective-permute-done | bytes 2336 | tf_op jit(solution)/shard_map/ppermute | solution.py:15
  47.8 3.8 %collective-permute-done.7 = f32[2,16,18,1]{3,2,1,0:T(8,128)S(1)} collective-permute-done((f32[2,16,18,1]{3,2,1,0:T(8,128)S(1)}, f32[2,16,18,1]{3,2,1,0:T(8,128)S(1)}, u32[]{:S(2)}, u32[]{:S(2)}) %collective-permute-start.7) | collective-permute-done | bytes 2336 | tf_op jit(solution)/shard_map/ppermute | solution.py:17
  53.5 3.3 %collective-permute-start.8 = (f32[2,16,1,256]{3,2,1,0:T(1,128)S(1)}, f32[2,16,1,256]{3,2,1,0:T(1,128)S(1)}, u32[]{:S(2)}, u32[]{:S(2)}) collective-permute-start(f32[2,16,1,256]{3,2,1,0:T(1,128)S(1)} %get-tuple-element.15), channel_id=1, source_target_pairs={{16,0},{32,16},{48,32},{64,48},{80,64},{96,80},{112,96},{128,112},... | collective-permute-start | bytes 98312 | tf_op jit(solution)/shard_map/ppermute | solution.py:17
  56.8 3.8 %collective-permute-start.9 = (f32[2,16,1,256]{3,2,1,0:T(1,128)S(1)}, f32[2,16,1,256]{3,2,1,0:T(1,128)S(1)}, u32[]{:S(2)}, u32[]{:S(2)}) collective-permute-start(f32[2,16,1,256]{3,2,1,0:T(1,128)S(1)} %get-tuple-element.16), channel_id=1, source_target_pairs={{0,16},{16,32},{32,48},{48,64},{64,80},{80,96},{96,112},{112,128},... | collective-permute-start | bytes 98312 | tf_op jit(solution)/shard_map/ppermute | solution.py:15
  63.2 5.1 %collective-permute-start.11 = (f32[2,16,18,1]{3,2,1,0:T(8,128)S(1)}, f32[2,16,18,1]{3,2,1,0:T(8,128)S(1)}, u32[]{:S(2)}, u32[]{:S(2)}) collective-permute-start(f32[2,16,18,1]{3,2,1,0:T(8,128)S(1)} %get-tuple-element.12), channel_id=1, source_target_pairs={{0,1},{1,2},{2,3},{3,4},{4,5},{5,6},{6,7},{7,8},{8,9},{9,10},{10,1... | collective-permute-start | bytes 6920 | tf_op jit(solution)/shard_map/ppermute | solution.py:15
  68.9 5.6 %collective-permute-done.10 = f32[2,16,18,1]{3,2,1,0:T(8,128)S(1)} collective-permute-done((f32[2,16,18,1]{3,2,1,0:T(8,128)S(1)}, f32[2,16,18,1]{3,2,1,0:T(8,128)S(1)}, u32[]{:S(2)}, u32[]{:S(2)}) %collective-permute-start.10) | collective-permute-done | bytes 2336 | tf_op jit(solution)/shard_map/ppermute | solution.py:17
  74.5 1.8 collective-permute-done.11
  78.5 59.8 %reduce-scatter.2.cloned.1.call-done = f32[1,16,16,256]{3,2,1,0:T(8,128)} async-done(((f32[2,16,16,256]{3,2,1,0:T(8,128)}), f32[1,16,16,256]{3,2,1,0:T(8,128)}) %reduce-scatter.2.cloned.1.call-update) | async-done | bytes 262160 | tf_op jit(solution)/shard_map/reduce_scatter | solution.py:102
  139.3 1.6 stack.8
  140.8 6.5 %all-to-all-start = ((bf16[16,16,16,256]{3,2,1,0:T(8,128)(2,1)}), bf16[16,16,16,256]{3,2,1,0:T(8,128)(2,1)S(1)}, u32[]{:S(2)}, u32[]{:S(2)}) async-start(bf16[16,16,16,256]{3,2,1,0:T(8,128)(2,1)} %stack.8), calls=%async_computation.1 | async-start | bytes 4194304 | tf_op jit(solution)/shard_map/all_to_all | solution.py:106
  147.5 1.9 select_maximum_fusion
  149.5 1.7 fusion.9
  151.2 24.3 %all-to-all-done = bf16[16,16,16,256]{3,2,1,0:T(8,128)(2,1)S(1)} async-done(((bf16[16,16,16,256]{3,2,1,0:T(8,128)(2,1)}), bf16[16,16,16,256]{3,2,1,0:T(8,128)(2,1)S(1)}, u32[]{:S(2)}, u32[]{:S(2)}) %all-to-all-start) | async-done | bytes 2097184 | tf_op jit(solution)/shard_map/all_to_all | solution.py:106
  175.5 2.5 copy.18
  178.0 2.7 %reshape.96 = bf16[16,16,32,128,1]{3,2,1,0,4:T(8,128)(2,1)S(1)} reshape(bf16[16,16,16,256]{3,2,1,0:T(8,128)(2,1)} %copy.18) | data formatting | bytes 4194304 | tf_op jit(solution)/shard_map/reshape;reshape | solution.py:109
  184.2 60.4 %all-reduce.5.cloned.1.call-done = f32[16,16,256]{2,1,0:T(8,128)} async-done(((f32[16,16,256]{2,1,0:T(8,128)}), f32[16,16,256]{2,1,0:T(8,128)}) %all-reduce.5.cloned.1.call-update) | async-done | bytes 262160 | tf_op jit(solution)/shard_map/psum | solution.py:118
  244.7 1.7 copy.30
  (98 shorter events, 22.4 us)
Async XLA Ops:
  7.2 174.1 %copy-start = (bf16[2,7,128,128]{3,2,1,0:T(8,128)(2,1)S(1)}, bf16[2,7,128,128]{3,2,1,0:T(8,128)(2,1)}, u32[]{:S(2)}) copy-start(bf16[2,7,128,128]{3,2,1,0:T(8,128)(2,1)} %param.18) | copy-start | bytes 1376260
  7.2 20.1 %copy-start.4 = (f32[16,16,256]{2,1,0:T(8,128)S(1)}, f32[16,16,256]{2,1,0:T(8,128)}, u32[]{:S(2)}) copy-start(f32[16,16,256]{2,1,0:T(8,128)} %param.12) | copy-start | bytes 786436
  7.2 19.8 %copy-start.21 = (s32[16,16,256]{2,1,0:T(8,128)S(1)}, s32[16,16,256]{2,1,0:T(8,128)}, u32[]{:S(2)}) copy-start(s32[16,16,256]{2,1,0:T(8,128)} %param.14) | copy-start | bytes 786436
  7.2 20.1 %copy-start.24 = (f32[2,2,8]{2,1,0:T(2,128)S(1)}, f32[2,2,8]{2,1,0:T(2,128)}, u32[]{:S(2)}) copy-start(f32[2,2,8]{2,1,0:T(2,128)} %param.16) | copy-start | bytes 388
  7.2 131.1 %reduce-scatter.2.cloned.1.call-start = ((), (), s32[]{:S(2)}) async-start(), calls=%async_computation.2 | async-start | bytes 786432 | tf_op jit(solution)/shard_map/reduce_scatter | solution.py:102
  8.3 18.9 %collective-permute-start.2 = (f32[16,1,256]{2,1,0:T(1,128)S(1)}, f32[16,1,256]{2,1,0:T(1,128)S(1)}, u32[]{:S(2)}, u32[]{:S(2)}) collective-permute-start(f32[16,1,256]{2,1,0:T(1,128)S(1)} %get-tuple-element.29), channel_id=1, source_target_pairs={{0,16},{16,32},{32,48},{48,64},{64,80},{80,96},{96,112},{112,128},... | collective-permute-start | bytes 49160 | tf_op jit(solution)/shard_map/ppermute | solution.py:15
  13.3 14.0 %collective-permute-start.3 = (f32[16,1,256]{2,1,0:T(1,128)S(1)}, f32[16,1,256]{2,1,0:T(1,128)S(1)}, u32[]{:S(2)}, u32[]{:S(2)}) collective-permute-start(f32[16,1,256]{2,1,0:T(1,128)S(1)} %get-tuple-element.30), channel_id=1, source_target_pairs={{16,0},{32,16},{48,32},{64,48},{80,64},{96,80},{112,96},{128,112},... | collective-permute-start | bytes 49160 | tf_op jit(solution)/shard_map/ppermute | solution.py:17
  19.5 17.6 %collective-permute-start = (f32[2,16,1,256]{3,2,1,0:T(1,128)S(1)}, f32[2,16,1,256]{3,2,1,0:T(1,128)S(1)}, u32[]{:S(2)}, u32[]{:S(2)}) collective-permute-start(f32[2,16,1,256]{3,2,1,0:T(1,128)S(1)} %get-tuple-element.19), channel_id=1, source_target_pairs={{16,0},{32,16},{48,32},{64,48},{80,64},{96,80},{112,96},{128,112},... | collective-permute-start | bytes 98312 | tf_op jit(solution)/shard_map/ppermute | solution.py:17
  21.4 15.7 %collective-permute-start.1 = (f32[2,16,1,256]{3,2,1,0:T(1,128)S(1)}, f32[2,16,1,256]{3,2,1,0:T(1,128)S(1)}, u32[]{:S(2)}, u32[]{:S(2)}) collective-permute-start(f32[2,16,1,256]{3,2,1,0:T(1,128)S(1)} %get-tuple-element.20), channel_id=1, source_target_pairs={{0,16},{16,32},{32,48},{48,64},{64,80},{80,96},{96,112},{112,128},... | collective-permute-start | bytes 98312 | tf_op jit(solution)/shard_map/ppermute | solution.py:15
  27.5 5.1 %collective-permute-start.4 = (f32[16,18,1]{2,1,0:T(8,128)S(1)}, f32[16,18,1]{2,1,0:T(8,128)S(1)}, u32[]{:S(2)}, u32[]{:S(2)}) collective-permute-start(f32[16,18,1]{2,1,0:T(8,128)S(1)} %get-tuple-element.22), channel_id=1, source_target_pairs={{0,1},{1,2},{2,3},{3,4},{4,5},{5,6},{6,7},{7,8},{8,9},{9,10},{10,1... | collective-permute-start | bytes 3464 | tf_op jit(solution)/shard_map/ppermute | solution.py:15
  28.9 7.8 %collective-permute-start.5 = (f32[16,18,1]{2,1,0:T(8,128)S(1)}, f32[16,18,1]{2,1,0:T(8,128)S(1)}, u32[]{:S(2)}, u32[]{:S(2)}) collective-permute-start(f32[16,18,1]{2,1,0:T(8,128)S(1)} %get-tuple-element.21), channel_id=1, source_target_pairs={{1,0},{2,1},{3,2},{4,3},{5,4},{6,5},{7,6},{8,7},{9,8},{10,9},{11,1... | collective-permute-start | bytes 3464 | tf_op jit(solution)/shard_map/ppermute | solution.py:17
  37.4 10.4 %collective-permute-start.6 = (f32[2,16,18,1]{3,2,1,0:T(8,128)S(1)}, f32[2,16,18,1]{3,2,1,0:T(8,128)S(1)}, u32[]{:S(2)}, u32[]{:S(2)}) collective-permute-start(f32[2,16,18,1]{3,2,1,0:T(8,128)S(1)} %get-tuple-element.14), channel_id=1, source_target_pairs={{0,1},{1,2},{2,3},{3,4},{4,5},{5,6},{6,7},{7,8},{8,9},{9,10},{10,1... | collective-permute-start | bytes 6920 | tf_op jit(solution)/shard_map/ppermute | solution.py:15
  39.6 12.0 %collective-permute-start.7 = (f32[2,16,18,1]{3,2,1,0:T(8,128)S(1)}, f32[2,16,18,1]{3,2,1,0:T(8,128)S(1)}, u32[]{:S(2)}, u32[]{:S(2)}) collective-permute-start(f32[2,16,18,1]{3,2,1,0:T(8,128)S(1)} %get-tuple-element.13), channel_id=1, source_target_pairs={{1,0},{2,1},{3,2},{4,3},{5,4},{6,5},{7,6},{8,7},{9,8},{10,9},{11,1... | collective-permute-start | bytes 6920 | tf_op jit(solution)/shard_map/ppermute | solution.py:17
  41.5 10.9 %copy-start.5 = (f32[16,16,256]{2,1,0:T(8,128)}, f32[16,16,256]{2,1,0:T(8,128)S(1)}, u32[]{:S(2)}) copy-start(f32[16,16,256]{2,1,0:T(8,128)S(1)} %get-tuple-element.23) | copy-start | bytes 786436
  41.5 10.9 %copy-start.7 = (f32[16,16,256]{2,1,0:T(8,128)}, f32[16,16,256]{2,1,0:T(8,128)S(1)}, u32[]{:S(2)}) copy-start(f32[16,16,256]{2,1,0:T(8,128)S(1)} %get-tuple-element.24) | copy-start | bytes 786436
  41.5 10.9 %copy-start.9 = (f32[16,16,256]{2,1,0:T(8,128)}, f32[16,16,256]{2,1,0:T(8,128)S(1)}, u32[]{:S(2)}) copy-start(f32[16,16,256]{2,1,0:T(8,128)S(1)} %get-tuple-element.25) | copy-start | bytes 786436
  41.5 10.9 %copy-start.11 = (f32[16,16,256]{2,1,0:T(8,128)}, f32[16,16,256]{2,1,0:T(8,128)S(1)}, u32[]{:S(2)}) copy-start(f32[16,16,256]{2,1,0:T(8,128)S(1)} %get-tuple-element.26) | copy-start | bytes 786436
  53.5 7.1 %collective-permute-start.8 = (f32[2,16,1,256]{3,2,1,0:T(1,128)S(1)}, f32[2,16,1,256]{3,2,1,0:T(1,128)S(1)}, u32[]{:S(2)}, u32[]{:S(2)}) collective-permute-start(f32[2,16,1,256]{3,2,1,0:T(1,128)S(1)} %get-tuple-element.15), channel_id=1, source_target_pairs={{16,0},{32,16},{48,32},{64,48},{80,64},{96,80},{112,96},{128,112},... | collective-permute-start | bytes 98312 | tf_op jit(solution)/shard_map/ppermute | solution.py:17
  56.8 11.5 %copy-start.17 = (bf16[2,2,16,16,256]{4,3,2,1,0:T(8,128)(2,1)S(1)}, bf16[2,2,16,16,256]{4,3,2,1,0:T(8,128)(2,1)}, u32[]{:S(2)}) copy-start(bf16[2,2,16,16,256]{4,3,2,1,0:T(8,128)(2,1)} %param.11) | copy-start | bytes 1572868
  56.8 4.8 %collective-permute-start.9 = (f32[2,16,1,256]{3,2,1,0:T(1,128)S(1)}, f32[2,16,1,256]{3,2,1,0:T(1,128)S(1)}, u32[]{:S(2)}, u32[]{:S(2)}) collective-permute-start(f32[2,16,1,256]{3,2,1,0:T(1,128)S(1)} %get-tuple-element.16), channel_id=1, source_target_pairs={{0,16},{16,32},{32,48},{48,64},{64,80},{80,96},{96,112},{112,128},... | collective-permute-start | bytes 98312 | tf_op jit(solution)/shard_map/ppermute | solution.py:15
  61.9 12.6 %collective-permute-start.10 = (f32[2,16,18,1]{3,2,1,0:T(8,128)S(1)}, f32[2,16,18,1]{3,2,1,0:T(8,128)S(1)}, u32[]{:S(2)}, u32[]{:S(2)}) collective-permute-start(f32[2,16,18,1]{3,2,1,0:T(8,128)S(1)} %get-tuple-element.11), channel_id=1, source_target_pairs={{1,0},{2,1},{3,2},{4,3},{5,4},{6,5},{7,6},{8,7},{9,8},{10,9},{11,1... | collective-permute-start | bytes 6920 | tf_op jit(solution)/shard_map/ppermute | solution.py:17
  63.2 13.0 %collective-permute-start.11 = (f32[2,16,18,1]{3,2,1,0:T(8,128)S(1)}, f32[2,16,18,1]{3,2,1,0:T(8,128)S(1)}, u32[]{:S(2)}, u32[]{:S(2)}) collective-permute-start(f32[2,16,18,1]{3,2,1,0:T(8,128)S(1)} %get-tuple-element.12), channel_id=1, source_target_pairs={{0,1},{1,2},{2,3},{3,4},{4,5},{5,6},{6,7},{7,8},{8,9},{9,10},{10,1... | collective-permute-start | bytes 6920 | tf_op jit(solution)/shard_map/ppermute | solution.py:15
  140.8 34.7 %all-to-all-start = ((bf16[16,16,16,256]{3,2,1,0:T(8,128)(2,1)}), bf16[16,16,16,256]{3,2,1,0:T(8,128)(2,1)S(1)}, u32[]{:S(2)}, u32[]{:S(2)}) async-start(bf16[16,16,16,256]{3,2,1,0:T(8,128)(2,1)} %stack.8), calls=%async_computation.1 | async-start | bytes 4194304 | tf_op jit(solution)/shard_map/all_to_all | solution.py:106
  147.4 97.3 %all-reduce.5.cloned.1.call-start = ((), (), s32[]{:S(2)}) async-start(), calls=%async_computation.3 | async-start | bytes 524288 | tf_op jit(solution)/shard_map/psum | solution.py:118
  (16 other events, 54.2 us)
Sparse Core Ops, SparseCore 0:
  78.7 59.6 reduce-scatter.1
  183.2 61.3 all-reduce.4
